TPU v7x, 32 devices: a whole 2x2x4 slice. The times are simulated.
32 devices in a mesh: stn: 8 (over z, x), chan: 4 (over y, core).
Axes of the slice: x: 2, y: 2, z: 4, core: 2. Of those that a mesh axis runs over, the one named last changes fastest.
Arguments:
- samples: bfloat16 [64, 17, 2, 8192], P(('stn', 'chan')), may hold values from -6 to 6
- keeper: int32 [8, 8], replicated, may hold values from 0 to 1, as said below
Outputs:
- visibilities: bfloat16 [64, 2, 4096, 40], P('stn', None, 'chan')
Inputs may be any that keep to these rules, and one draw needn't show every extreme that they name: keeper[g, g] is 1; for g != h with d = (g - h) mod 8: keeper[g, h] is 1 where 0 < d < 4, 0 where d > 4, and at d = 4 exactly one of keeper[g, h] and keeper[h, g] is 1, which one drawn for each such pair; half of the rows hold 5 ones, the others 5 - 1.
All inputs are finite; a program needn't handle non-finite values.
Results may differ from a plain program's by a relative error of at most 0.0077.
Values may be sent and summed in bfloat16 or wider, within the bound.
A program may use at most 192 MiB of HBM per device.

v0:
```python
import math

import jax
import jax.numpy as jnp
from jax import lax
from jax.sharding import PartitionSpec as P

NFFT = 8192
TAPS = 16
CH_WIN = 1024
DFT_BLOCK = 256


def from_behind(value, axis, by):
    devices = lax.axis_size(axis)
    return lax.ppermute(value, axis, [(i, (i + by) % devices) for i in range(devices)])


def taps_table():
    pos = jnp.arange(TAPS * NFFT).astype(jnp.float32)
    shifted = (pos + 0.5) / NFFT - TAPS / 2.0
    window = 0.5 - 0.5 * jnp.cos(2.0 * math.pi * (pos + 0.5) / (TAPS * NFFT))
    return (jnp.sinc(shifted) * window).reshape(TAPS, NFFT)


def twiddles(width):
    index_n = jnp.arange(NFFT, dtype=jnp.int32)[:, None]
    index_k = jnp.arange(width, dtype=jnp.int32)[None, :]
    phase = (index_n * index_k % NFFT).astype(jnp.float32) * (2.0 * math.pi / NFFT)
    cosines = jnp.cos(phase).astype(jnp.bfloat16)
    sines = jnp.sin(phase).astype(jnp.bfloat16)
    upper = jnp.concatenate([cosines, -sines], axis=1)
    lower = jnp.concatenate([sines, cosines], axis=1)
    return jnp.concatenate([upper, lower], axis=0)


def rotations(ch_tot, width):
    blocks = ch_tot // width
    index_n = jnp.arange(NFFT, dtype=jnp.int32)[None, :]
    index_b = jnp.arange(blocks, dtype=jnp.int32)[:, None]
    phase = (index_n * index_b * width % NFFT).astype(jnp.float32) * (2.0 * math.pi / NFFT)
    return (jnp.cos(phase), jnp.sin(phase))


def channelise(block, taps, table, cos_rot, sin_rot, ch_tot):
    frames = block.shape[1] - TAPS + 1
    count = block.shape[0]
    width = table.shape[1] // 2
    blocks = ch_tot // width
    total = taps[0] * block[:, 0:frames].astype(jnp.float32)
    for tap in range(1, TAPS):
        total = total + taps[tap] * block[:, tap : tap + frames].astype(jnp.float32)
    real_part = total[:, :, 0][None]
    imag_part = total[:, :, 1][None]
    cosine = cos_rot[:, None, None, :]
    sine = sin_rot[:, None, None, :]
    rot_real = real_part * cosine + imag_part * sine
    rot_imag = imag_part * cosine - real_part * sine
    lhs = jnp.stack([rot_real, rot_imag], axis=3).astype(jnp.bfloat16)
    lhs = lhs.reshape(blocks * count * frames, 2 * NFFT)
    spectrum = jnp.dot(lhs, table, preferred_element_type=jnp.float32) * (1.0 / math.sqrt(NFFT))
    spectrum = spectrum.astype(jnp.bfloat16).reshape(blocks, count, frames, 2, width)
    spectrum = jnp.transpose(spectrum, (1, 0, 4, 3, 2))
    return spectrum.reshape(count, ch_tot, 2, frames)


def correlate(own, others, frames):
    half = others.shape[2] // 2
    turned = jnp.concatenate([-others[:, :, half:], others[:, :, :half]], axis=2)
    rhs = jnp.concatenate([others, turned], axis=0)
    product = lax.dot_general(
        own, rhs, (((2,), (2,)), ((1,), (1,))), preferred_element_type=jnp.float32
    )
    rows = others.shape[0]
    product = product.reshape(product.shape[0], product.shape[1], 2, rows)
    return jnp.transpose(product, (1, 2, 0, 3)) / frames


def slot_table(keep_rows, keep_slots):
    ranking = jnp.cumsum(keep_rows, axis=1) - 1
    slot_index = jnp.arange(keep_slots, dtype=jnp.int32)
    matched = (keep_rows[:, :, None] == 1) & (ranking[:, :, None] == slot_index[None, None, :])
    column_ids = jnp.arange(keep_rows.shape[1], dtype=jnp.int32)
    slot_column = jnp.sum(jnp.where(matched, column_ids[None, :, None], 0), axis=1)
    filled = jnp.any(matched, axis=1)
    return (slot_column, filled)


def per_device(samples, keeper):
    n_chan = lax.axis_size("chan")
    n_stn = lax.axis_size("stn")
    ch_tot = CH_WIN * n_chan
    frames = samples.shape[1] - TAPS + 1
    cos_rot, sin_rot = rotations(ch_tot, DFT_BLOCK)
    spectrum = channelise(samples, taps_table(), twiddles(DFT_BLOCK), cos_rot, sin_rot, ch_tot)
    local = lax.all_to_all(spectrum, "chan", split_axis=1, concat_axis=0, tiled=True)
    group_in = local.shape[0]
    own = local.reshape(group_in, CH_WIN, 2 * frames)
    keep_slots = n_stn // 2 + 1
    group_index = lax.axis_index("stn")
    row_keep = jnp.take(keeper, group_index, axis=0)
    slot_column, filled = slot_table(row_keep[None], keep_slots)
    slot_column = slot_column[0]
    filled = filled[0]
    nothing = jnp.zeros((), jnp.bfloat16)
    half = n_stn // 2
    stacked = own[None]
    stride = 1
    while stride < half:
        moved = from_behind(stacked, "stn", stride)
        stacked = jnp.concatenate([stacked, moved], axis=0)
        stride = stride * 2
    far_group = from_behind(own, "stn", half)
    partners = jnp.concatenate([stacked, far_group[None]], axis=0)
    partners = partners.reshape((half + 1) * group_in, CH_WIN, 2 * frames)
    tiles = correlate(own, partners, frames).astype(jnp.bfloat16)
    tiles = tiles.reshape(group_in, 2, CH_WIN, half + 1, group_in)
    slot_distance = jnp.minimum((group_index - slot_column) % n_stn, half)
    picked = jnp.take(tiles, slot_distance, axis=3)
    picked = jnp.where(filled[None, None, None, :, None], picked, nothing)
    return picked.reshape(group_in, 2, CH_WIN, keep_slots * group_in)


def solution(mesh):
    placed = (P(("stn", "chan"), None, None, None), P())
    return jax.shard_map(
        per_device,
        mesh=mesh,
        in_specs=placed,
        out_specs=P("stn", None, "chan", None),
        check_vma=False,
    )
```

profile of v0, /device:TPU:0, one launch (start us, length us, event | category | flops | bytes accessed | tf_op | source)
XLA Modules:
  0.0 166.4 jit_solution(14174221383164325046)
XLA Ops:
  0.0 2.4 %fusion.29 = f32[131072]{0:T(1024)S(1)} fusion(), kind=kLoop, calls=%fused_computation.45 | loop fusion | flops 5373952 | bytes 524288 | tf_op jit(solution)/shard_map/mul | solution.py:23
  2.4 2.1 %fusion.41 = (f32[16,8192]{1,0:T(8,128)S(1)}, f32[16,8192]{1,0:T(8,128)S(1)}) fusion(), kind=kLoop, calls=%fused_computation.65 | loop fusion | flops 1966080 | bytes 1048576 | tf_op jit(solution)/shard_map/sin | solution.py:42
  4.5 35.0 %sine_convert_fusion = (bf16[8192,256]{1,0:T(8,128)(2,1)}, bf16[8192,256]{1,0:T(8,128)(2,1)}) fusion(), kind=kLoop, calls=%fused_computation.15 | loop fusion | flops 33554432 | bytes 8388608 | tf_op jit(solution)/shard_map/convert_element_type | solution.py:31
  39.5 32.3 %fusion.14 = bf16[8192,256]{1,0:T(8,128)(2,1)} fusion(), kind=kLoop, calls=%fused_computation.24 | loop fusion | flops 37748736 | bytes 4194304 | tf_op jit(solution)/shard_map/neg | solution.py:32
  71.9 2.1 %multiply_add_fusion.1 = f32[2,2,2,8192]{3,2,1,0:T(2,128)S(1)} fusion(bf16[2,17,2,8192]{3,2,1,0:T(2,128)(2,1)S(1)} %copy-done, f32[8192]{0:T(1024)S(1)} %get-tuple-element.19, f32[8192]{0:T(1024)S(1)} %get-tuple-element.20, f32[8192]{0:T(1024)S(1)} %get-tuple-element.21, f32[8192]{0:T(1024)S(1)} %get-tuple-element.22, f32[8192]{0:T(1024)S(1)} %get-tuple-element.23, ...), kind=kLoop, calls=%fused_computation.67 | loop fusion | flops 3080192 | bytes 2883584 | tf_op jit(solution)/shard_map/add | solution.py:52
  74.4 4.4 %add_convert_fusion = (bf16[16,2,2,1,8192]{4,3,2,1,0:T(2,128)(2,1)S(1)}, bf16[16,2,2,1,8192]{4,3,2,1,0:T(2,128)(2,1)S(1)}) fusion(f32[16,8192]{1,0:T(8,128)S(1)} %get-tuple-element.40, f32[2,2,8192]{2,1,0:T(2,128)S(1)} %get-tuple-element.38, f32[16,8192]{1,0:T(8,128)S(1)} %get-tuple-element.41, f32[2,2,8192]{2,1,0:T(2,128)S(1)} %get-tuple-element.39), kind=kLoop, calls=%fused_computation.23 | loop fusion | flops 4194304 | bytes 3407872 | tf_op jit(solution)/shard_map/convert
  78.8 4.8 %pad_maximum_fusion = bf16[16,2,2,2,8192]{4,3,2,1,0:T(2,128)(2,1)S(1)} fusion(bf16[16,2,2,1,8192]{4,3,2,1,0:T(2,128)(2,1)S(1)} %get-tuple-element.17, bf16[16,2,2,1,8192]{4,3,2,1,0:T(2,128)(2,1)S(1)} %get-tuple-element.16), kind=kLoop, calls=%fused_computation.21 | loop fusion | flops 4194304 | bytes 4194304 | tf_op jit(solution)/shard_map/stack | solution.py:59
  84.8 13.7 %fusion.19 = bf16[64,512]{1,0:T(8,128)(2,1)S(1)} fusion(bf16[64,16384]{1,0:T(8,128)(2,1)S(1)} %bitcast.50, bf16[8192,256]{1,0:T(8,128)(2,1)} %get-tuple-element.43, bf16[8192,256]{1,0:T(8,128)(2,1)} %get-tuple-element.42, bf16[8192,256]{1,0:T(8,128)(2,1)} %fusion.14), kind=kOutput, calls=%fused_computation.28 | convolution fusion | flops 1140916224 | bytes 14745600 | tf_op jit(solution)/shard_map/dot_general | solution.py:61
  98.6 4.9 %copy.50 = bf16[2,16,256,2,2]{4,3,0,2,1:T(2,128)(2,1)} copy(bf16[2,16,256,2,2]{2,1,4,3,0:T(8,128)(2,1)S(1)} %bitcast.51) | data formatting | bytes 131072 | tf_op jit(solution)/shard_map/reshape | solution.py:64
  103.6 7.8 %reshape.394 = bf16[4,2,4096]{2,1,0:T(2,128)(2,1)} reshape(bf16[4096,2,2,2]{3,2,1,0:T(2,128)(2,1)} %bitcast.46) | data formatting | bytes 131072
  111.3 4.3 %all-to-all-start = ((bf16[4,2,4096]{2,1,0:T(2,128)(2,1)}), bf16[4,2,4096]{2,1,0:T(2,128)(2,1)S(1)}, u32[]{:S(2)}, u32[]{:S(2)}) async-start(bf16[4,2,4096]{2,1,0:T(2,128)(2,1)} %reshape.394), calls=%async_computation | async-start | bytes 131072 | tf_op jit(solution)/shard_map/all_to_all | solution.py:96
  117.4 2.3 %all-to-all-done = bf16[4,2,4096]{2,1,0:T(2,128)(2,1)S(1)} async-done(((bf16[4,2,4096]{2,1,0:T(2,128)(2,1)}), bf16[4,2,4096]{2,1,0:T(2,128)(2,1)S(1)}, u32[]{:S(2)}, u32[]{:S(2)}) %all-to-all-start) | async-done | bytes 65568 | tf_op jit(solution)/shard_map/all_to_all | solution.py:96
  119.7 10.0 %reshape.395 = bf16[4096,2,2,2]{3,2,1,0:T(2,128)(2,1)} reshape(bf16[4,2,4096]{2,1,0:T(2,128)(2,1)S(1)} %all-to-all-done) | data formatting | bytes 131072
  129.7 9.7 %copy.51 = bf16[2,4,1024,2,2]{2,1,4,3,0:T(4,128)(2,1)S(1)} copy(bf16[2,4,1024,2,2]{4,3,0,2,1:T(2,128)(2,1)} %bitcast.47) | data formatting | bytes 131072 | tf_op jit(solution)/shard_map/all_to_all | solution.py:96
  139.6 2.0 %collective-permute-start = (bf16[1,8,1024,4]{2,1,3,0:T(8,128)(2,1)S(1)}, bf16[1,8,1024,4]{2,1,3,0:T(8,128)(2,1)S(1)}, u32[]{:S(2)}, u32[]{:S(2)}) collective-permute-start(bf16[1,8,1024,4]{2,1,3,0:T(8,128)(2,1)S(1)} %broadcast_in_dim_reshape.3), channel_id=1, source_target_pairs={{0,4},{4,8},{8,12},{12,16},{16,20},{20,24},{24,28},{28,0},{1,5},{5... | collective-permute-start | bytes 196616 | tf_op jit(solution)/shard_map/ppermute | solution.py:16
  141.6 5.3 %collective-permute-done = bf16[1,8,1024,4]{2,1,3,0:T(8,128)(2,1)S(1)} collective-permute-done((bf16[1,8,1024,4]{2,1,3,0:T(8,128)(2,1)S(1)}, bf16[1,8,1024,4]{2,1,3,0:T(8,128)(2,1)S(1)}, u32[]{:S(2)}, u32[]{:S(2)}) %collective-permute-start) | collective-permute-done | bytes 65568 | tf_op jit(solution)/shard_map/ppermute | solution.py:16
  147.5 2.6 %collective-permute-start.2 = (bf16[8,1024,4]{1,0,2:T(8,128)(2,1)S(1)}, bf16[8,1024,4]{1,0,2:T(8,128)(2,1)S(1)}, u32[]{:S(2)}, u32[]{:S(2)}) collective-permute-start(bf16[8,1024,4]{1,0,2:T(8,128)(2,1)S(1)} %reshape.350), channel_id=1, source_target_pairs={{0,16},{4,20},{8,24},{12,28},{16,0},{20,4},{24,8},{28,12},{1,17},{... | collective-permute-start | bytes 196616 | tf_op jit(solution)/shard_map/ppermute | solution.py:16
  150.1 1.4 copy.46
  151.5 4.0 %collective-permute-done.2 = bf16[8,1024,4]{1,0,2:T(8,128)(2,1)S(1)} collective-permute-done((bf16[8,1024,4]{1,0,2:T(8,128)(2,1)S(1)}, bf16[8,1024,4]{1,0,2:T(8,128)(2,1)S(1)}, u32[]{:S(2)}, u32[]{:S(2)}) %collective-permute-start.2) | collective-permute-done | bytes 65568 | tf_op jit(solution)/shard_map/ppermute | solution.py:16
  155.5 1.4 copy.44
  157.0 1.4 copy.45
  158.4 3.8 %multiply_convert_fusion = bf16[1024,8,80]{2,1,0:T(8,128)(2,1)S(1)} fusion(bf16[8,1024,4]{0,2,1:T(4,128)(2,1)} %copy.46, bf16[40,1024,4]{0,2,1:T(4,128)(2,1)} %copy.45, bf16[40,1024,4]{0,2,1:T(4,128)(2,1)} %copy.44), kind=kOutput, calls=%fused_computation.20 | convolution fusion | flops 7864320 | bytes 2031616 | tf_op jit(solution)/shard_map/dot_general | solution.py:71
  162.2 2.0 %copy.47 = bf16[1024,8,80]{0,2,1:T(8,128)(2,1)S(1)} copy(bf16[1024,8,80]{2,1,0:T(8,128)(2,1)S(1)} %multiply_convert_fusion) | data formatting | bytes 2621440 | tf_op jit(solution)/shard_map/convert_element_type | solution.py:116
  165.0 1.5 fusion.15
  (32 shorter events, 5.0 us)
Async XLA Ops:
  39.5 32.4 %copy-start = (bf16[2,17,2,8192]{3,2,1,0:T(2,128)(2,1)S(1)}, bf16[2,17,2,8192]{3,2,1,0:T(2,128)(2,1)}, u32[]{:S(2)}) copy-start(bf16[2,17,2,8192]{3,2,1,0:T(2,128)(2,1)} %param.2) | copy-start | bytes 3342340
  111.3 8.4 %all-to-all-start = ((bf16[4,2,4096]{2,1,0:T(2,128)(2,1)}), bf16[4,2,4096]{2,1,0:T(2,128)(2,1)S(1)}, u32[]{:S(2)}, u32[]{:S(2)}) async-start(bf16[4,2,4096]{2,1,0:T(2,128)(2,1)} %reshape.394), calls=%async_computation | async-start | bytes 131072 | tf_op jit(solution)/shard_map/all_to_all | solution.py:96
  139.6 7.3 %collective-permute-start = (bf16[1,8,1024,4]{2,1,3,0:T(8,128)(2,1)S(1)}, bf16[1,8,1024,4]{2,1,3,0:T(8,128)(2,1)S(1)}, u32[]{:S(2)}, u32[]{:S(2)}) collective-permute-start(bf16[1,8,1024,4]{2,1,3,0:T(8,128)(2,1)S(1)} %broadcast_in_dim_reshape.3), channel_id=1, source_target_pairs={{0,4},{4,8},{8,12},{12,16},{16,20},{20,24},{24,28},{28,0},{1,5},{5... | collective-permute-start | bytes 196616 | tf_op jit(solution)/shard_map/ppermute | solution.py:16
  146.9 8.6 %collective-permute-start.1 = (bf16[2,8,1024,4]{2,1,3,0:T(8,128)(2,1)S(1)}, bf16[2,8,1024,4]{2,1,3,0:T(8,128)(2,1)S(1)}, u32[]{:S(2)}, u32[]{:S(2)}) collective-permute-start(bf16[2,8,1024,4]{2,1,3,0:T(8,128)(2,1)S(1)} %pad_maximum_fusion.3), channel_id=1, source_target_pairs={{0,8},{4,12},{8,16},{12,20},{16,24},{20,28},{24,0},{28,4},{1,9},{5... | collective-permute-start | bytes 393224 | tf_op jit(solution)/shard_map/ppermute | solution.py:16
  147.5 8.0 %collective-permute-start.2 = (bf16[8,1024,4]{1,0,2:T(8,128)(2,1)S(1)}, bf16[8,1024,4]{1,0,2:T(8,128)(2,1)S(1)}, u32[]{:S(2)}, u32[]{:S(2)}) collective-permute-start(bf16[8,1024,4]{1,0,2:T(8,128)(2,1)S(1)} %reshape.350), channel_id=1, source_target_pairs={{0,16},{4,20},{8,24},{12,28},{16,0},{20,4},{24,8},{28,12},{1,17},{... | collective-permute-start | bytes 196616 | tf_op jit(solution)/shard_map/ppermute | solution.py:16
where the time goes:
time: 167 us; the launch traced here: 166 us
  other arithmetic  86.7 us (52%)
  local copies, waits for them, and re-layouts  41.5 us (25%)
  matrix products  17.5 us (10%)
  waiting for transfers between devices  11.6 us (7%)
  starting transfers between devices  8.94 us (5%)
    convert_element_type x1, other arithmetic, twiddles(): sines = jnp.sin(phase).astype(jnp.bfloat16)  35 us
    neg x1, other arithmetic, twiddles(): upper = jnp.concatenate([cosines, -sines], axis=1)  32.3 us
    unnamed x6, local copies, waits for them, and re-layouts  19.2 us
    dot_general x1, matrix products, channelise(): jnp.dot(lhs, table, preferred_element_type=jnp.float32)  13.7 us
    all_to_all x2, local copies, waits for them, and re-layouts, per_device(): lax.all_to_all(spectrum, 'chan', split_axis=1, concat_axis=0, tiled=True)  9.8 us
    ppermute x3, waiting for transfers between devices, from_behind(): lax.ppermute(value, axis, [(i, (i + by) % devices) for i in range(devices)])  9.25 us
    reshape x1, local copies, waits for them, and re-layouts, channelise(): return spectrum.reshape(count, ch_tot, 2, frames)  4.94 us
    another operation x1, other arithmetic, channelise(): lhs = jnp.stack([rot_real, rot_imag], axis=3).astype(jnp.bfloat16)  4.84 us
  transfers between devices with their start and end apart: 4, of which 3 were waited for; matrix products, arithmetic and copies ran while one was open for 2% of the time, Pallas kernels for 0%

commit v1 on v0

v1 whole, which is shorter than its diff:
```python
import functools
import math

import jax
import jax.numpy as jnp
import numpy as np
from jax import lax
from jax.experimental import pallas as pl
from jax.experimental.pallas import tpu as pltpu
from jax.sharding import PartitionSpec as P

TAPS = 16
LANES = 128
CH_WIN = 1024
HIGH = lax.Precision.HIGHEST


def tables(nfft, n_k2):
    n_1 = nfft // LANES
    pos = np.arange(TAPS * nfft, dtype=np.float64)
    window = 0.5 - 0.5 * np.cos(2.0 * np.pi * (pos + 0.5) / (TAPS * nfft))
    taps = np.sinc((pos + 0.5) / nfft - TAPS / 2.0) * window
    taps = np.repeat(taps.reshape(TAPS, n_1, LANES), 2, axis=1)
    k_1 = np.arange(n_1)
    n_2 = np.arange(LANES)
    angle = 2.0 * np.pi * (k_1[:, None] * k_1[None, :] % n_1) / n_1
    cosine, sine = np.cos(angle), np.sin(angle)
    first = np.zeros((2, n_1, n_1, 2))
    first[0, :, :, 0] = cosine
    first[0, :, :, 1] = sine
    first[1, :, :, 0] = -sine
    first[1, :, :, 1] = cosine
    first = first.reshape(2 * n_1, 2 * n_1)
    angle = 2.0 * np.pi * (n_2[:, None] * k_1[None, :] % nfft) / nfft
    scale = 1.0 / math.sqrt(nfft)
    turn_c = np.concatenate([np.cos(angle), np.cos(angle)], axis=1) * scale
    turn_s = np.concatenate([np.sin(angle), -np.sin(angle)], axis=1) * scale
    k_2 = np.concatenate([np.arange(0, n_k2, 2), np.arange(1, n_k2, 2)])
    angle = 2.0 * np.pi * (k_2[:, None] * n_2[None, :] % LANES) / LANES
    second = np.concatenate([np.cos(angle), np.sin(angle)], axis=1)
    return [np.asarray(a, np.float32) for a in (taps, first, turn_c, turn_s, second)]


def filter_rows(x_ref, taps_ref, held, inputs, frames):
    rows = taps_ref.shape[1]
    chunk = 16
    for start in range(0, rows, chunk):
        part = slice(start, start + chunk)
        for i in range(inputs):
            totals = [None] * frames
            for step in range(TAPS + frames - 1):
                value = x_ref[i, step, part, :].astype(jnp.float32)
                for f in range(frames):
                    if 0 <= step - f < TAPS:
                        term = value * taps_ref[step - f, part, :]
                        totals[f] = term if totals[f] is None else totals[f] + term
            for f in range(frames):
                seq = i * frames + f
                held[part, seq * LANES : (seq + 1) * LANES] = totals[f]


def transform(held, first_ref, turn_c_ref, turn_s_ref, second_ref, seqs):
    half = LANES // 2
    stage = jnp.dot(first_ref[...], held[...], precision=HIGH, preferred_element_type=jnp.float32)
    lane = lax.broadcasted_iota(jnp.int32, (LANES, LANES), 1)
    sign = jnp.where(lane < half, 1.0, -1.0)
    tops, lows = [], []
    for seq in range(seqs):
        turned = stage[:, seq * LANES : (seq + 1) * LANES].T
        turned = turned * turn_c_ref[...] + pltpu.roll(turned, half, 1) * turn_s_ref[...]
        tops.append(turned)
        lows.append(pltpu.roll(turned, half, 1) * sign)
    rhs = jnp.concatenate([jnp.concatenate(tops, axis=1), jnp.concatenate(lows, axis=1)], axis=0)
    spectra = jnp.dot(second_ref[...], rhs, precision=HIGH, preferred_element_type=jnp.float32)
    tiles = spectra.shape[0] // 2
    low_lane = lax.broadcasted_iota(jnp.int32, (tiles, LANES), 1) < half
    planes = []
    for seq in range(seqs):
        even = spectra[:tiles, seq * LANES : (seq + 1) * LANES]
        odd = spectra[tiles:, seq * LANES : (seq + 1) * LANES]
        real = jnp.where(low_lane, even, pltpu.roll(odd, half, 1))
        imag = jnp.where(low_lane, pltpu.roll(even, half, 1), odd)
        planes.append((real, imag))
    return planes


def channel_kernel(x_ref, taps_ref, first_ref, turn_c_ref, turn_s_ref, second_ref, out_ref, held):
    inputs, frames = out_ref.shape[1], out_ref.shape[2]
    n_chan, tiles = out_ref.shape[0], out_ref.shape[4]
    filter_rows(x_ref, taps_ref, held, inputs, frames)
    planes = transform(held, first_ref, turn_c_ref, turn_s_ref, second_ref, inputs * frames)
    for i in range(inputs):
        for f in range(frames):
            for p in range(2):
                plane = planes[i * frames + f][p].astype(jnp.bfloat16)
                for d in range(n_chan):
                    out_ref[d, i, f, p] = plane[d * tiles : (d + 1) * tiles]


def channelise(samples, n_chan):
    inputs, frames_in, _, nfft = samples.shape
    frames = frames_in - TAPS + 1
    tiles = CH_WIN // LANES
    n_1 = nfft // LANES
    consts = tables(nfft, CH_WIN * n_chan // n_1)
    x = samples.reshape(inputs, frames_in, 2, n_1, LANES)
    x = jnp.transpose(x, (0, 1, 3, 2, 4)).reshape(inputs, frames_in, 2 * n_1, LANES)
    return pl.pallas_call(
        channel_kernel,
        out_shape=jax.ShapeDtypeStruct((n_chan, inputs, frames, 2, tiles, LANES), jnp.bfloat16),
        in_specs=[pl.BlockSpec(memory_space=pltpu.VMEM)] * 6,
        out_specs=pl.BlockSpec(memory_space=pltpu.VMEM),
        scratch_shapes=[pltpu.VMEM((2 * n_1, inputs * frames * LANES), jnp.float32)],
        name="channelise",
    )(x, *consts)


def correlate_kernel(width, dist_ref, fill_ref, parts_ref, out_ref, rhs):
    step = pl.program_id(0)
    _, inputs, frames, _, tiles, _ = parts_ref.shape
    slots = dist_ref.shape[0]

    @pl.when(step == 0)
    def _():
        rhs[...] = jnp.zeros_like(rhs)
        for s in range(slots):
            d = dist_ref[s]
            gain = fill_ref[s]
            for f in range(frames):
                block = []
                for p in range(2):
                    value = parts_ref[d, :, f, p].astype(jnp.float32) * gain
                    block.append(jnp.transpose(value, (1, 0, 2)))
                real, imag = block
                real_col = slice(2 * f * LANES, (2 * f + 1) * LANES)
                imag_col = slice((2 * f + 1) * LANES, (2 * f + 2) * LANES)
                top = slice(s * inputs, (s + 1) * inputs)
                low = slice(width + s * inputs, width + (s + 1) * inputs)
                rhs[:, top, real_col] = real.astype(jnp.bfloat16)
                rhs[:, top, imag_col] = imag.astype(jnp.bfloat16)
                rhs[:, low, real_col] = (-imag).astype(jnp.bfloat16)
                rhs[:, low, imag_col] = real.astype(jnp.bfloat16)

    row_id = lax.broadcasted_iota(jnp.int32, (LANES, LANES), 0)
    col_id = lax.broadcasted_iota(jnp.int32, (LANES, LANES), 1)
    eye = jnp.where(row_id == col_id, 1.0, 0.0).astype(jnp.bfloat16)
    sub_id = lax.broadcasted_iota(jnp.int32, (tiles, LANES), 0)
    weights = rhs[step]
    for i in range(inputs):
        diags = []
        for f in range(frames):
            for p in range(2):
                rows = parts_ref[0, i, f, p].astype(jnp.float32)
                row = jnp.sum(jnp.where(sub_id == step, rows, 0.0), axis=0, keepdims=True)
                wide = jnp.broadcast_to(row, (LANES, LANES)).astype(jnp.bfloat16)
                diags.append(wide * eye)
        product = lax.dot_general(
            jnp.concatenate(diags, axis=1),
            weights,
            (((1,), (1,)), ((), ())),
            preferred_element_type=jnp.float32,
        )
        cols = out_ref.shape[3]
        out_ref[i, 0] = product[:, :cols].astype(jnp.bfloat16)
        out_ref[i, 1] = product[:, width : width + cols].astype(jnp.bfloat16)


def correlate(parts, dist, gain):
    _, inputs, frames, _, tiles, _ = parts.shape
    slots = dist.shape[0]
    cols = slots * inputs
    width = -(-cols // LANES) * LANES
    return pl.pallas_call(
        functools.partial(correlate_kernel, width),
        out_shape=jax.ShapeDtypeStruct((inputs, 2, tiles * LANES, cols), jnp.bfloat16),
        grid=(tiles,),
        in_specs=[
            pl.BlockSpec(memory_space=pltpu.SMEM),
            pl.BlockSpec(memory_space=pltpu.SMEM),
            pl.BlockSpec(parts.shape, lambda t: (0,) * 6),
        ],
        out_specs=pl.BlockSpec((inputs, 2, LANES, cols), lambda t: (0, 0, t, 0)),
        scratch_shapes=[pltpu.VMEM((tiles, 2 * width, 2 * frames * LANES), jnp.bfloat16)],
        name="correlate",
    )(dist, gain, parts)


def slot_table(keep_row, keep_slots):
    ranking = jnp.cumsum(keep_row) - 1
    slot_index = jnp.arange(keep_slots, dtype=jnp.int32)
    matched = (keep_row[:, None] == 1) & (ranking[:, None] == slot_index[None, :])
    column_ids = jnp.arange(keep_row.shape[0], dtype=jnp.int32)
    slot_column = jnp.sum(jnp.where(matched, column_ids[:, None], 0), axis=0)
    filled = jnp.any(matched, axis=0)
    return slot_column, filled


def from_behind(value, axis, by):
    devices = lax.axis_size(axis)
    return lax.ppermute(value, axis, [(i, (i + by) % devices) for i in range(devices)])


def per_device(samples, keeper):
    n_chan = lax.axis_size("chan")
    n_stn = lax.axis_size("stn")
    half = n_stn // 2
    frames = samples.shape[1] - TAPS + 1
    group = lax.axis_index("stn")
    slot_column, filled = slot_table(jnp.take(keeper, group, axis=0), half + 1)
    dist = jnp.minimum((group - slot_column) % n_stn, half).astype(jnp.int32)
    gain = jnp.where(filled, 1.0 / frames, 0.0).astype(jnp.float32)

    spectrum = channelise(samples, n_chan)
    own = lax.all_to_all(spectrum, "chan", split_axis=0, concat_axis=0, tiled=True)
    own = own.reshape((own.shape[0] * own.shape[1],) + own.shape[2:])
    stacked = own[None]
    stride = 1
    while stride < half:
        moved = from_behind(stacked, "stn", stride)
        stacked = jnp.concatenate([stacked, moved], axis=0)
        stride = stride * 2
    far_group = from_behind(own, "stn", half)
    parts = jnp.concatenate([stacked, far_group[None]], axis=0)
    return correlate(parts, dist, gain)


def solution(mesh):
    placed = (P(("stn", "chan"), None, None, None), P())
    return jax.shard_map(
        per_device,
        mesh=mesh,
        in_specs=placed,
        out_specs=P("stn", None, "chan", None),
        check_vma=False,
    )
```

time: 167 us -> 40.9 us (0.24)
  other arithmetic: 86.7 us -> 3.61 us
  local copies, waits for them, and re-layouts: 41.5 us -> 4.61 us
  matrix products: 17.5 us -> 0 us
  Pallas kernels: 0 us -> 12.4 us
    convert_element_type x1 -> x0, other arithmetic: 35 us -> none  [twiddles(): sines = jnp.sin(phase).astype(jnp.bfloat16)]
    neg x2 -> x0, other arithmetic: 32.4 us -> none  [the longest x1 32.3 us: twiddles(): upper = jnp.concatenate([cosines, -sines], axis=1)]
    unnamed x6 -> x0, local copies, waits for them, and re-layouts: 19.2 us -> none
    dot_general x2 -> x0, matrix products: 17.5 us -> none  [the longest x1 13.7 us: channelise(): jnp.dot(lhs, table, preferred_element_type=jnp.float32)]
    pallas_call x0 -> x2, Pallas kernels: none -> 12.4 us  [the longest x1 8.72 us: correlate(): pl.pallas_call(functools.partial(correlate_kernel, width), out_shape=jax....]
    all_to_all x2 -> x0, local copies, waits for them, and re-layouts: 9.8 us -> none  [per_device(): lax.all_to_all(spectrum, 'chan', split_axis=1, concat_axis=0, tiled=True)]
    another operation x3 -> x1, other arithmetic: 9.42 us -> 0.18 us  [the longest x1 4.84 us: channelise(): lhs = jnp.stack([rot_real, rot_imag], axis=3).astype(jnp.bfloat16)]
    reshape x7 -> x0, local copies, waits for them, and re-layouts: 7.89 us -> none  [the longest x1 4.94 us: channelise(): return spectrum.reshape(count, ch_tot, 2, frames)]
  transfers between devices with their start and end apart: 4 -> 4, of which waited for: 3 -> 3; matrix products, arithmetic and copies ran while one was open for 2% -> 7% of each run, Pallas kernels for 0% -> 0%
where the time goes in v1:
time: 40.9 us; the launch traced here: 40.5 us
  Pallas kernels  12.4 us (30%)
  waiting for transfers between devices  11 us (27%)
  starting transfers between devices  8.92 us (22%)
  local copies, waits for them, and re-layouts  4.61 us (11%)
  other arithmetic  3.61 us (9%)
    ppermute x3, waiting for transfers between devices, from_behind(): lax.ppermute(value, axis, [(i, (i + by) % devices) for i in range(devices)])  9.05 us
    pallas_call x1, Pallas kernels, correlate(): pl.pallas_call(functools.partial(correlate_kernel, width), out_shape=jax....  8.72 us
    ppermute x3, starting transfers between devices, from_behind(): lax.ppermute(value, axis, [(i, (i + by) % devices) for i in range(devices)])  4.66 us
    pallas_call x1, local copies, waits for them, and re-layouts, correlate(): pl.pallas_call(functools.partial(correlate_kernel, width), out_shape=jax....  4.61 us
    all_to_all x1, starting transfers between devices, per_device(): lax.all_to_all(spectrum, 'chan', split_axis=0, concat_axis=0, tiled=True)  4.26 us
    pallas_call x1, Pallas kernels, channelise(): pl.pallas_call(channel_kernel, out_shape=jax.ShapeDtypeStruct((n_chan, in...  3.7 us
    all_to_all x1, waiting for transfers between devices, per_device(): lax.all_to_all(spectrum, 'chan', split_axis=0, concat_axis=0, tiled=True)  1.92 us
  transfers between devices with their start and end apart: 4, of which 3 were waited for; matrix products, arithmetic and copies ran while one was open for 7% of the time, Pallas kernels for 0%

profile of v1, /device:TPU:0, one launch (start us, length us, event | category | flops | bytes accessed | tf_op | source)
XLA Modules:
  0.0 40.5 jit_solution(16673093389192595317)
XLA Ops:
  0.0 3.7 %channelise.1 = bf16[4,2,2,2,8,128]{5,4,3,2,1,0:T(8,128)(2,1)} custom-call(bf16[2,17,128,128]{3,2,1,0:T(8,128)(2,1)} %bitcast.14, f32[16,128,128]{2,1,0:T(8,128)} %constant.63.clone.taps_ref, f32[128,128]{1,0:T(8,128)} %constant.64.clone.first_ref, f32[128,128]{1,0:T(8,128)} %constant.65.clone.turn_c_ref, f32[128,128]{1,0:T(8,128)} %constant.66.clone.turn_s_ref, ...), custom_call_target="tpu_custom_call" | custom-call | tf_op jit(solution)/shard_map/channelise/pallas_call | solution.py:108
  3.7 4.3 %all-to-all-start = ((bf16[4,2,2,2,8,128]{5,4,3,2,1,0:T(8,128)(2,1)}), bf16[4,2,2,2,8,128]{5,4,3,2,1,0:T(8,128)(2,1)S(1)}, u32[]{:S(2)}, u32[]{:S(2)}) async-start(bf16[4,2,2,2,8,128]{5,4,3,2,1,0:T(8,128)(2,1)} %channelise.1), calls=%async_computation | async-start | bytes 131072 | tf_op jit(solution)/shard_map/all_to_all | solution.py:214
  8.0 0.7 %compare_bitcast_fusion = pred[8]{0:T(512)(128)(4,1)S(1)} fusion(s32[8,8]{1,0:T(8,128)} %param.8, s32[]{:T(128)S(6)} %select_n.36, pred[]{:T(512)S(6)} %and.22), kind=kLoop, calls=%fused_computation.8 | loop fusion | flops 16 | bytes 45 | tf_op jit(solution)/shard_map/eq | solution.py:191
  8.7 0.7 %fusion.4 = s32[8,1]{0,1:T(1,128)S(1)} fusion(s32[8,8]{1,0:T(8,128)} %param.8, s32[]{:T(128)S(6)} %select_n.36, pred[]{:T(512)S(6)} %and.22), kind=kLoop, calls=%fused_computation.15 | loop fusion | flops 8 | bytes 69 | tf_op jit(solution)/shard_map/jit(_take)/select_n | solution.py:209
  9.4 0.2 reduce-window.8
  9.5 0.1 select_reduce_fusion
  9.6 0.5 %fusion.2.dist_ref = s32[5]{0:T(128)} fusion(s32[5]{0:T(128)S(1)} %select_reduce_fusion, s32[]{:T(128)S(6)} %axis_index.15), kind=kLoop, calls=%fused_computation.11 | loop fusion | flops 65 | bytes 44 | tf_op jit(solution)/shard_map/min | solution.py:210
  10.2 1.9 %all-to-all-done = bf16[4,2,2,2,8,128]{5,4,3,2,1,0:T(8,128)(2,1)S(1)} async-done(((bf16[4,2,2,2,8,128]{5,4,3,2,1,0:T(8,128)(2,1)}), bf16[4,2,2,2,8,128]{5,4,3,2,1,0:T(8,128)(2,1)S(1)}, u32[]{:S(2)}, u32[]{:S(2)}) %all-to-all-start) | async-done | bytes 65568 | tf_op jit(solution)/shard_map/all_to_all | solution.py:214
  12.1 2.0 %collective-permute-start = (bf16[1,8,2,2,8,128]{5,4,3,2,1,0:T(8,128)(2,1)S(1)}, bf16[1,8,2,2,8,128]{5,4,3,2,1,0:T(8,128)(2,1)S(1)}, u32[]{:S(2)}, u32[]{:S(2)}) collective-permute-start(bf16[1,8,2,2,8,128]{5,4,3,2,1,0:T(8,128)(2,1)S(1)} %bitcast.15), channel_id=1, source_target_pairs={{0,4},{4,8},{8,12},{12,16},{16,20},{20,24},{24,28},{28,0},{1,5},{5... | collective-permute-start | bytes 196616 | tf_op jit(solution)/shard_map/ppermute | solution.py:200
  14.0 0.1 fusion.1
  14.1 2.6 %collective-permute-start.2 = (bf16[8,2,2,8,128]{4,3,2,1,0:T(8,128)(2,1)S(1)}, bf16[8,2,2,8,128]{4,3,2,1,0:T(8,128)(2,1)S(1)}, u32[]{:S(2)}, u32[]{:S(2)}) collective-permute-start(bf16[8,2,2,8,128]{4,3,2,1,0:T(8,128)(2,1)S(1)} %bitcast.16), channel_id=1, source_target_pairs={{0,16},{4,20},{8,24},{12,28},{16,0},{20,4},{24,8},{28,12},{1,17},{... | collective-permute-start | bytes 196616 | tf_op jit(solution)/shard_map/ppermute | solution.py:200
  16.8 2.8 %collective-permute-done = bf16[1,8,2,2,8,128]{5,4,3,2,1,0:T(8,128)(2,1)S(1)} collective-permute-done((bf16[1,8,2,2,8,128]{5,4,3,2,1,0:T(8,128)(2,1)S(1)}, bf16[1,8,2,2,8,128]{5,4,3,2,1,0:T(8,128)(2,1)S(1)}, u32[]{:S(2)}, u32[]{:S(2)}) %collective-permute-start) | collective-permute-done | bytes 65568 | tf_op jit(solution)/shard_map/ppermute | solution.py:200
  19.6 0.1 collective-permute-start.1
  19.7 0.5 %broadcast_select_fusion.1.fill_ref = f32[5]{0:T(128)} fusion(pred[5]{0:T(512)(128)(4,1)S(1)} %fusion.1), kind=kLoop, calls=%fused_computation.14 | loop fusion | flops 5 | bytes 25 | tf_op jit(solution)/shard_map/jit(_where)/select_n | solution.py:211
  20.2 0.0 collective-permute-done.2
  20.2 6.2 %collective-permute-done.1 = bf16[2,8,2,2,8,128]{5,4,3,2,1,0:T(8,128)(2,1)S(1)} collective-permute-done((bf16[2,8,2,2,8,128]{5,4,3,2,1,0:T(8,128)(2,1)S(1)}, bf16[2,8,2,2,8,128]{5,4,3,2,1,0:T(8,128)(2,1)S(1)}, u32[]{:S(2)}, u32[]{:S(2)}) %collective-permute-start.1) | collective-permute-done | bytes 131104 | tf_op jit(solution)/shard_map/ppermute | solution.py:200
  26.4 0.8 %pad_maximum_fusion.parts_ref = bf16[5,8,2,2,8,128]{5,4,3,2,1,0:T(8,128)(2,1)} fusion(bf16[1,8,2,2,8,128]{5,4,3,2,1,0:T(8,128)(2,1)S(1)} %bitcast.19, bf16[2,8,2,2,8,128]{5,4,3,2,1,0:T(8,128)(2,1)S(1)} %collective-permute-done.1, bf16[1,8,2,2,8,128]{5,4,3,2,1,0:T(8,128)(2,1)S(1)} %collective-permute-done, bf16[1,8,2,2,8,128]{5,4,3,2,1,0:T(8,128)(2,1)S(1)} %bitcast.18), kind=kLoop, calls=%fused_computation | loop fusion | flops 491520 | bytes 655360 | tf_op jit(solution)/shard_map/concatenate | solution.py:223
  27.2 8.7 %correlate.1 = bf16[8,2,1024,40]{3,2,1,0:T(8,128)(2,1)} custom-call(s32[5]{0:T(128)} %fusion.2.dist_ref, f32[5]{0:T(128)} %broadcast_select_fusion.1.fill_ref, bf16[5,8,2,2,8,128]{5,4,3,2,1,0:T(8,128)(2,1)} %pad_maximum_fusion.parts_ref), custom_call_target="tpu_custom_call" | custom-call | tf_op jit(solution)/shard_map/correlate/pallas_call | solution.py:173
  35.9 4.6 %copy.11 = bf16[8,2,1024,40]{2,3,1,0:T(8,128)(2,1)} copy(bf16[8,2,1024,40]{3,2,1,0:T(8,128)(2,1)} %correlate.1) | data formatting | bytes 2621440 | tf_op jit(solution)/shard_map/correlate/pallas_call | solution.py:173
  (2 shorter events, 0.0 us)
Async XLA Ops:
  3.7 8.4 %all-to-all-start = ((bf16[4,2,2,2,8,128]{5,4,3,2,1,0:T(8,128)(2,1)}), bf16[4,2,2,2,8,128]{5,4,3,2,1,0:T(8,128)(2,1)S(1)}, u32[]{:S(2)}, u32[]{:S(2)}) async-start(bf16[4,2,2,2,8,128]{5,4,3,2,1,0:T(8,128)(2,1)} %channelise.1), calls=%async_computation | async-start | bytes 131072 | tf_op jit(solution)/shard_map/all_to_all | solution.py:214
  12.1 7.5 %collective-permute-start = (bf16[1,8,2,2,8,128]{5,4,3,2,1,0:T(8,128)(2,1)S(1)}, bf16[1,8,2,2,8,128]{5,4,3,2,1,0:T(8,128)(2,1)S(1)}, u32[]{:S(2)}, u32[]{:S(2)}) collective-permute-start(bf16[1,8,2,2,8,128]{5,4,3,2,1,0:T(8,128)(2,1)S(1)} %bitcast.15), channel_id=1, source_target_pairs={{0,4},{4,8},{8,12},{12,16},{16,20},{20,24},{24,28},{28,0},{1,5},{5... | collective-permute-start | bytes 196616 | tf_op jit(solution)/shard_map/ppermute | solution.py:200
  14.1 6.1 %collective-permute-start.2 = (bf16[8,2,2,8,128]{4,3,2,1,0:T(8,128)(2,1)S(1)}, bf16[8,2,2,8,128]{4,3,2,1,0:T(8,128)(2,1)S(1)}, u32[]{:S(2)}, u32[]{:S(2)}) collective-permute-start(bf16[8,2,2,8,128]{4,3,2,1,0:T(8,128)(2,1)S(1)} %bitcast.16), channel_id=1, source_target_pairs={{0,16},{4,20},{8,24},{12,28},{16,0},{20,4},{24,8},{28,12},{1,17},{... | collective-permute-start | bytes 196616 | tf_op jit(solution)/shard_map/ppermute | solution.py:200
  19.6 6.8 %collective-permute-start.1 = (bf16[2,8,2,2,8,128]{5,4,3,2,1,0:T(8,128)(2,1)S(1)}, bf16[2,8,2,2,8,128]{5,4,3,2,1,0:T(8,128)(2,1)S(1)}, u32[]{:S(2)}, u32[]{:S(2)}) collective-permute-start(bf16[2,8,2,2,8,128]{5,4,3,2,1,0:T(8,128)(2,1)S(1)} %pad_maximum_fusion.1), channel_id=1, source_target_pairs={{0,8},{4,12},{8,16},{12,20},{16,24},{20,28},{24,0},{28,4},{1,9},{5... | collective-permute-start | bytes 393224 | tf_op jit(solution)/shard_map/ppermute | solution.py:200

commit v2 on v1

v2 whole, which is shorter than its diff:
```python
import math

import jax
import jax.numpy as jnp
import numpy as np
from jax import lax
from jax.experimental import pallas as pl
from jax.experimental.pallas import tpu as pltpu
from jax.sharding import PartitionSpec as P

TAPS = 16
LANES = 128
CH_WIN = 1024
HIGH = lax.Precision.HIGHEST
OUT_SPACE = pl.ANY


def tables(nfft, n_k2):
    n_1 = nfft // LANES
    pos = np.arange(TAPS * nfft, dtype=np.float64)
    window = 0.5 - 0.5 * np.cos(2.0 * np.pi * (pos + 0.5) / (TAPS * nfft))
    taps = np.sinc((pos + 0.5) / nfft - TAPS / 2.0) * window
    taps = np.repeat(taps.reshape(TAPS, n_1, LANES), 2, axis=1)
    k_1 = np.arange(n_1)
    n_2 = np.arange(LANES)
    angle = 2.0 * np.pi * (k_1[:, None] * k_1[None, :] % n_1) / n_1
    cosine, sine = np.cos(angle), np.sin(angle)
    first = np.zeros((2, n_1, n_1, 2))
    first[0, :, :, 0] = cosine
    first[0, :, :, 1] = sine
    first[1, :, :, 0] = -sine
    first[1, :, :, 1] = cosine
    first = first.reshape(2 * n_1, 2 * n_1)
    angle = 2.0 * np.pi * (n_2[:, None] * k_1[None, :] % nfft) / nfft
    scale = 1.0 / math.sqrt(nfft)
    turn_c = np.concatenate([np.cos(angle), np.cos(angle)], axis=1) * scale
    turn_s = np.concatenate([np.sin(angle), -np.sin(angle)], axis=1) * scale
    k_2 = np.concatenate([np.arange(0, n_k2, 2), np.arange(1, n_k2, 2)])
    angle = 2.0 * np.pi * (k_2[:, None] * n_2[None, :] % LANES) / LANES
    second = np.concatenate([np.cos(angle), np.sin(angle)], axis=1)
    return [np.asarray(a, np.float32) for a in (taps, first, turn_c, turn_s, second)]


def filter_rows(x_ref, taps_ref, held, inputs, frames):
    rows = taps_ref.shape[1]
    chunk = 16
    for start in range(0, rows, chunk):
        part = slice(start, start + chunk)
        for i in range(inputs):
            totals = [None] * frames
            for step in range(TAPS + frames - 1):
                value = x_ref[i, step, part, :].astype(jnp.float32)
                for f in range(frames):
                    if 0 <= step - f < TAPS:
                        term = value * taps_ref[step - f, part, :]
                        totals[f] = term if totals[f] is None else totals[f] + term
            for f in range(frames):
                seq = i * frames + f
                held[part, seq * LANES : (seq + 1) * LANES] = totals[f]


def transform(held, first_ref, turn_c_ref, turn_s_ref, second_ref, seqs):
    half = LANES // 2
    stage = jnp.dot(first_ref[...], held[...], precision=HIGH, preferred_element_type=jnp.float32)
    lane = lax.broadcasted_iota(jnp.int32, (LANES, LANES), 1)
    sign = jnp.where(lane < half, 1.0, -1.0)
    tops, lows = [], []
    for seq in range(seqs):
        turned = stage[:, seq * LANES : (seq + 1) * LANES].T
        turned = turned * turn_c_ref[...] + pltpu.roll(turned, half, 1) * turn_s_ref[...]
        tops.append(turned)
        lows.append(pltpu.roll(turned, half, 1) * sign)
    rhs = jnp.concatenate([jnp.concatenate(tops, axis=1), jnp.concatenate(lows, axis=1)], axis=0)
    spectra = jnp.dot(second_ref[...], rhs, precision=HIGH, preferred_element_type=jnp.float32)
    tiles = spectra.shape[0] // 2
    low_lane = lax.broadcasted_iota(jnp.int32, (tiles, LANES), 1) < half
    planes = []
    for seq in range(seqs):
        even = spectra[:tiles, seq * LANES : (seq + 1) * LANES]
        odd = spectra[tiles:, seq * LANES : (seq + 1) * LANES]
        real = jnp.where(low_lane, even, pltpu.roll(odd, half, 1))
        imag = jnp.where(low_lane, pltpu.roll(even, half, 1), odd)
        planes.append((real, imag))
    return planes


def send_kernel(
    x_ref, taps_ref, first_ref, turn_c_ref, turn_s_ref, second_ref, parts_ref, held, mine, here_sem, send_sem, pass_sem, recv_sem
):
    n_chan, inputs, frames, _, tiles, _ = mine.shape
    n_stn = lax.axis_size("stn")
    hops = (parts_ref.shape[0] - 1) // 2
    stn = lax.axis_index("stn")
    chan = lax.axis_index("chan")
    odd = lax.rem(stn, 2)
    pair = stn + 1 - 2 * odd

    barrier = pltpu.get_barrier_semaphore()
    for j in range(hops + 1):
        for step in range(n_chan):
            if j or step:
                there = (lax.rem(stn + n_stn - 2 * j, n_stn), lax.rem(chan + step, n_chan))
                pl.semaphore_signal(barrier, inc=1, device_id=there, device_id_type=pl.DeviceIdType.MESH)
    pl.semaphore_signal(barrier, inc=1, device_id=(pair, chan), device_id_type=pl.DeviceIdType.MESH)

    filter_rows(x_ref, taps_ref, held, inputs, frames)
    planes = transform(held, first_ref, turn_c_ref, turn_s_ref, second_ref, inputs * frames)
    for i in range(inputs):
        for f in range(frames):
            for p in range(2):
                plane = planes[i * frames + f][p].astype(jnp.bfloat16)
                for d in range(n_chan):
                    mine[d, i, f, p] = plane[d * tiles : (d + 1) * tiles]
    pl.semaphore_wait(barrier, (hops + 1) * n_chan)

    def direct(j, step):
        to = lax.rem(chan + step, n_chan)
        return pltpu.make_async_remote_copy(
            src_ref=mine.at[to],
            dst_ref=parts_ref.at[2 * j, chan],
            send_sem=send_sem.at[j, step],
            recv_sem=recv_sem.at[2 * j, chan],
            device_id=(lax.rem(stn + 2 * j, n_stn), to),
            device_id_type=pl.DeviceIdType.MESH,
        )

    def arrival(distance, origin):
        return pltpu.make_async_remote_copy(
            src_ref=mine.at[0],
            dst_ref=parts_ref.at[distance, origin],
            send_sem=send_sem.at[0, 0],
            recv_sem=recv_sem.at[distance, origin],
            device_id=(pair, chan),
            device_id_type=pl.DeviceIdType.MESH,
        )

    def passed(j, step):
        origin = lax.rem(chan + step, n_chan)
        return pltpu.make_async_remote_copy(
            src_ref=parts_ref.at[2 * (j + odd), origin],
            dst_ref=parts_ref.at[2 * j + 1, origin],
            send_sem=pass_sem.at[j, step],
            recv_sem=recv_sem.at[2 * j + 1, origin],
            device_id=(pair, chan),
            device_id_type=pl.DeviceIdType.MESH,
        )

    keep = pltpu.make_async_copy(mine.at[chan], parts_ref.at[0, chan], here_sem)
    keep.start()
    for step in range(n_chan):
        for j in range(hops, -1, -1):
            if j or step:
                direct(j, step).start()
    keep.wait()
    for j in range(hops + 1):
        for step in range(n_chan):
            if j or step:
                arrival(2 * j, lax.rem(chan + n_chan - step, n_chan)).wait_recv()
        first = j == 0
        last = j == hops

        @pl.when(odd == 0)
        def _():
            if not last:
                for step in range(n_chan):
                    passed(j, step).start()

        @pl.when(odd == 1)
        def _():
            if not first:
                for step in range(n_chan):
                    passed(j - 1, step).start()

    for j in range(hops):
        for step in range(n_chan):
            arrival(2 * j + 1, lax.rem(chan + step, n_chan)).wait_recv()
            passed(j, step).wait_send()
    for j in range(hops + 1):
        for step in range(n_chan):
            if j or step:
                direct(j, step).wait_send()


def channelise(samples, n_chan, half):
    inputs, frames_in, _, nfft = samples.shape
    frames = frames_in - TAPS + 1
    tiles = CH_WIN // LANES
    n_1 = nfft // LANES
    consts = tables(nfft, CH_WIN * n_chan // n_1)
    x = samples.reshape(inputs, frames_in, 2, n_1, LANES)
    x = jnp.transpose(x, (0, 1, 3, 2, 4)).reshape(inputs, frames_in, 2 * n_1, LANES)
    piece = (n_chan, inputs, frames, 2, tiles, LANES)
    return pl.pallas_call(
        send_kernel,
        out_shape=jax.ShapeDtypeStruct((half + 1,) + piece, jnp.bfloat16),
        in_specs=[pl.BlockSpec(memory_space=pltpu.VMEM)] * 6,
        out_specs=pl.BlockSpec(memory_space=OUT_SPACE),
        scratch_shapes=[
            pltpu.VMEM((2 * n_1, inputs * frames * LANES), jnp.float32),
            pltpu.VMEM(piece, jnp.bfloat16),
            pltpu.SemaphoreType.DMA,
            pltpu.SemaphoreType.DMA((half // 2 + 1, n_chan)),
            pltpu.SemaphoreType.DMA((half // 2, n_chan)),
            pltpu.SemaphoreType.DMA((half + 1, n_chan)),
        ],
        compiler_params=pltpu.CompilerParams(collective_id=0, has_side_effects=True),
        name="channelise",
    )(x, *consts)


def correlate_kernel(keeper_ref, parts_ref, out_ref, own, others, dist, gain):
    step = pl.program_id(0)
    _, n_chan, pieces, frames, _, tiles, _ = parts_ref.shape
    inputs = n_chan * pieces
    slots = parts_ref.shape[0]
    n_stn = keeper_ref.shape[0]

    @pl.when(step == 0)
    def _():
        group = lax.axis_index("stn")
        for s in range(slots):
            dist[s] = 0
            gain[s] = jnp.float32(0.0)

        def place(h, rank):
            kept = keeper_ref[group, h] == 1

            @pl.when(kept & (rank < slots))
            def _():
                dist[rank] = jnp.minimum(lax.rem(group + n_stn - h, n_stn), slots - 1)
                gain[rank] = jnp.float32(1.0 / frames)

            return rank + kept.astype(jnp.int32)

        lax.fori_loop(0, n_stn, place, jnp.int32(0))

        for f in range(frames):
            for p in range(2):
                value = parts_ref[0, :, :, f, p].astype(jnp.float32).reshape(inputs, tiles, LANES)
                own[f, p] = jnp.transpose(value, (1, 0, 2))
                for s in range(slots):
                    value = parts_ref[dist[s], :, :, f, p].astype(jnp.float32) * gain[s]
                    value = value.reshape(inputs, tiles, LANES)
                    others[f, p, s] = jnp.transpose(value, (1, 0, 2))

    for t in range(tiles):
        rows = []
        for i in range(pieces):
            rows.append([
                [jnp.broadcast_to(own[f, p, t, pl.ds(step * pieces + i, 1), :], (inputs, LANES)) for p in range(2)]
                for f in range(frames)
            ])
        for s in range(slots):
            block = [[others[f, p, s, t] for p in range(2)] for f in range(frames)]
            for i in range(pieces):
                real, imag = 0.0, 0.0
                for f in range(frames):
                    a_re, a_im = rows[i][f]
                    b_re, b_im = block[f]
                    real = real + (a_re * b_re + a_im * b_im)
                    imag = imag + (a_im * b_re - a_re * b_im)
                top = slice(s * inputs, (s + 1) * inputs)
                col = slice(t * LANES, (t + 1) * LANES)
                out_ref[i, 0, top, col] = real.astype(jnp.bfloat16)
                out_ref[i, 1, top, col] = imag.astype(jnp.bfloat16)


def correlate(keeper, parts):
    slots, n_chan, pieces, frames, _, tiles, _ = parts.shape
    inputs = n_chan * pieces
    out = pl.pallas_call(
        correlate_kernel,
        out_shape=jax.ShapeDtypeStruct((inputs, 2, slots * inputs, tiles * LANES), jnp.bfloat16),
        grid=(n_chan,),
        in_specs=[
            pl.BlockSpec(memory_space=pltpu.SMEM),
            pl.BlockSpec(parts.shape, lambda t: (0,) * 7),
        ],
        out_specs=pl.BlockSpec((pieces, 2, slots * inputs, tiles * LANES), lambda t: (t, 0, 0, 0)),
        scratch_shapes=[
            pltpu.VMEM((frames, 2, tiles, inputs, LANES), jnp.float32),
            pltpu.VMEM((frames, 2, slots, tiles, inputs, LANES), jnp.float32),
            pltpu.SMEM((slots,), jnp.int32),
            pltpu.SMEM((slots,), jnp.float32),
        ],
        name="correlate",
    )(keeper, parts)
    return jnp.transpose(out, (0, 1, 3, 2))


def per_device(samples, keeper):
    half = lax.axis_size("stn") // 2
    return correlate(keeper, channelise(samples, lax.axis_size("chan"), half))


def solution(mesh):
    placed = (P(("stn", "chan"), None, None, None), P())
    return jax.shard_map(
        per_device,
        mesh=mesh,
        in_specs=placed,
        out_specs=P("stn", None, "chan", None),
        check_vma=False,
    )
```

time: 40.9 us -> 21.9 us (0.54)
  waiting for transfers between devices: 11 us -> 0 us
  Pallas kernels: 12.4 us -> 21.8 us
  starting transfers between devices: 8.92 us -> 0 us
  local copies, waits for them, and re-layouts: 4.61 us -> 0 us
  other arithmetic: 3.61 us -> 0 us
    pallas_call x2, Pallas kernels: 12.4 us -> 21.8 us  [the longest x1 18.5 us: channelise(): pl.pallas_call(send_kernel, out_shape=jax.ShapeDtypeStruct((half + 1,) +...]
    ppermute x3 -> x0, waiting for transfers between devices: 9.05 us -> none  [from_behind(): lax.ppermute(value, axis, [(i, (i + by) % devices) for i in range(devices)])]
    ppermute x3 -> x0, starting transfers between devices: 4.66 us -> none  [from_behind(): lax.ppermute(value, axis, [(i, (i + by) % devices) for i in range(devices)])]
    pallas_call x1 -> x0, local copies, waits for them, and re-layouts: 4.61 us -> none  [correlate(): pl.pallas_call(functools.partial(correlate_kernel, width), out_shape=jax....]
    all_to_all x1 -> x0, starting transfers between devices: 4.26 us -> none  [per_device(): lax.all_to_all(spectrum, 'chan', split_axis=0, concat_axis=0, tiled=True)]
    all_to_all x1 -> x0, waiting for transfers between devices: 1.92 us -> none  [per_device(): lax.all_to_all(spectrum, 'chan', split_axis=0, concat_axis=0, tiled=True)]
    select_n x2 -> x0, other arithmetic: 1.24 us -> none  [the longest x1 0.69 us: per_device(): slot_column, filled = slot_table(jnp.take(keeper, group, axis=0), half + 1)]
    concatenate x2 -> x0, other arithmetic: 0.78 us -> none  [the longest x1 0.77 us: per_device(): parts = jnp.concatenate([stacked, far_group[None]], axis=0)]
  transfers between devices with their start and end apart: 4 -> 0, of which waited for: 3 -> 0; matrix products, arithmetic and copies ran while one was open for 7% -> 0% of each run, Pallas kernels for 0% -> 0%
where the time goes in v2:
time: 21.9 us; the launch traced here: 21.8 us
  Pallas kernels  21.8 us (100%)
    pallas_call x1, Pallas kernels, channelise(): pl.pallas_call(send_kernel, out_shape=jax.ShapeDtypeStruct((half + 1,) +...  18.5 us
    pallas_call x1, Pallas kernels, correlate(): pl.pallas_call(correlate_kernel, out_shape=jax.ShapeDtypeStruct((inputs,...  3.29 us

profile of v2, /device:TPU:0, one launch (start us, length us, event | category | flops | bytes accessed | tf_op | source)
XLA Modules:
  0.0 21.8 jit_solution(2888480664535374639)
XLA Ops:
  0.0 18.5 %channelise.1.parts_ref = bf16[5,4,2,2,2,8,128]{6,5,4,3,2,1,0:T(8,128)(2,1)} custom-call(bf16[2,17,128,128]{3,2,1,0:T(8,128)(2,1)} %bitcast.6, f32[16,128,128]{2,1,0:T(8,128)} %constant.10.clone.taps_ref, f32[128,128]{1,0:T(8,128)} %constant.11.clone.first_ref, f32[128,128]{1,0:T(8,128)} %constant.12.clone.turn_c_ref, f32[128,128]{1,0:T(8,128)} %constant.13.clone.turn_s_ref, ...), custom_call_target="tpu_custom_call" | custom-call | tf_op jit(solution)/shard_map/channelise/pallas_call | solution.py:193
  18.5 3.3 %correlate.1 = bf16[8,2,40,1024]{3,2,1,0:T(8,128)(2,1)} custom-call(s32[8,8]{1,0:T(8,128)} %keeper_ref.1, bf16[5,4,2,2,2,8,128]{6,5,4,3,2,1,0:T(8,128)(2,1)} %channelise.1.parts_ref), custom_call_target="tpu_custom_call" | custom-call | tf_op jit(solution)/shard_map/correlate/pallas_call | solution.py:271

commit v3 on v2

--- a/solution.py
+++ b/solution.py
@@ -41,22 +41,20 @@
     return [np.asarray(a, np.float32) for a in (taps, first, turn_c, turn_s, second)]
 
 
-def filter_rows(x_ref, taps_ref, held, inputs, frames):
+def filter_rows(x_ref, taps_ref, held, i, frames):
     rows = taps_ref.shape[1]
     chunk = 16
     for start in range(0, rows, chunk):
         part = slice(start, start + chunk)
-        for i in range(inputs):
-            totals = [None] * frames
-            for step in range(TAPS + frames - 1):
-                value = x_ref[i, step, part, :].astype(jnp.float32)
-                for f in range(frames):
-                    if 0 <= step - f < TAPS:
-                        term = value * taps_ref[step - f, part, :]
-                        totals[f] = term if totals[f] is None else totals[f] + term
+        totals = [None] * frames
+        for step in range(TAPS + frames - 1):
+            value = x_ref[i, step, part, :].astype(jnp.float32)
             for f in range(frames):
-                seq = i * frames + f
-                held[part, seq * LANES : (seq + 1) * LANES] = totals[f]
+                if 0 <= step - f < TAPS:
+                    term = value * taps_ref[step - f, part, :]
+                    totals[f] = term if totals[f] is None else totals[f] + term
+        for f in range(frames):
+            held[part, f * LANES : (f + 1) * LANES] = totals[f]
 
 
 def transform(held, first_ref, turn_c_ref, turn_s_ref, second_ref, seqs):
@@ -85,7 +83,7 @@
 
 
 def send_kernel(
-    x_ref, taps_ref, first_ref, turn_c_ref, turn_s_ref, second_ref, parts_ref, held, mine, here_sem, send_sem, pass_sem, recv_sem
+    x_ref, taps_ref, first_ref, turn_c_ref, turn_s_ref, second_ref, parts_ref, x, taps, held, mine, load_sem, here_sem, send_sem, pass_sem, recv_sem
 ):
     n_chan, inputs, frames, _, tiles, _ = mine.shape
     n_stn = lax.axis_size("stn")
@@ -103,24 +101,16 @@
                 pl.semaphore_signal(barrier, inc=1, device_id=there, device_id_type=pl.DeviceIdType.MESH)
     pl.semaphore_signal(barrier, inc=1, device_id=(pair, chan), device_id_type=pl.DeviceIdType.MESH)
 
-    filter_rows(x_ref, taps_ref, held, inputs, frames)
-    planes = transform(held, first_ref, turn_c_ref, turn_s_ref, second_ref, inputs * frames)
-    for i in range(inputs):
-        for f in range(frames):
-            for p in range(2):
-                plane = planes[i * frames + f][p].astype(jnp.bfloat16)
-                for d in range(n_chan):
-                    mine[d, i, f, p] = plane[d * tiles : (d + 1) * tiles]
-    pl.semaphore_wait(barrier, (hops + 1) * n_chan)
-
-    def direct(j, step):
-        to = lax.rem(chan + step, n_chan)
+    def place(turn):
+        return turn + odd * (hops - 2 * turn)
+
+    def direct(j, step, src, dst):
         return pltpu.make_async_remote_copy(
-            src_ref=mine.at[to],
-            dst_ref=parts_ref.at[2 * j, chan],
+            src_ref=src,
+            dst_ref=dst,
             send_sem=send_sem.at[j, step],
             recv_sem=recv_sem.at[2 * j, chan],
-            device_id=(lax.rem(stn + 2 * j, n_stn), to),
+            device_id=(lax.rem(stn + 2 * j, n_stn), lax.rem(chan + step, n_chan)),
             device_id_type=pl.DeviceIdType.MESH,
         )
 
@@ -134,51 +124,67 @@
             device_id_type=pl.DeviceIdType.MESH,
         )
 
-    def passed(j, step):
-        origin = lax.rem(chan + step, n_chan)
+    def passed(turn, step):
+        origin = lax.rem(chan + n_chan - step, n_chan)
+        j = place(turn)
+        there = 2 * j + 1 - 2 * odd
         return pltpu.make_async_remote_copy(
-            src_ref=parts_ref.at[2 * (j + odd), origin],
-            dst_ref=parts_ref.at[2 * j + 1, origin],
-            send_sem=pass_sem.at[j, step],
-            recv_sem=recv_sem.at[2 * j + 1, origin],
+            src_ref=parts_ref.at[2 * j, origin],
+            dst_ref=parts_ref.at[there, origin],
+            send_sem=pass_sem.at[turn, step],
+            recv_sem=recv_sem.at[there, origin],
             device_id=(pair, chan),
             device_id_type=pl.DeviceIdType.MESH,
         )
 
     keep = pltpu.make_async_copy(mine.at[chan], parts_ref.at[0, chan], here_sem)
+    copies = [pltpu.make_async_copy(taps_ref, taps, load_sem.at[inputs])]
+    copies += [pltpu.make_async_copy(x_ref.at[i], x.at[i], load_sem.at[i]) for i in range(inputs)]
+    for copy in copies:
+        copy.start()
+    copies[0].wait()
+    for i in range(inputs):
+        copies[i + 1].wait()
+        filter_rows(x, taps, held, i, frames)
+        planes = transform(held, first_ref, turn_c_ref, turn_s_ref, second_ref, frames)
+        for f in range(frames):
+            for p in range(2):
+                plane = planes[f][p].astype(jnp.bfloat16)
+                for d in range(n_chan):
+                    mine[d, i, f, p] = plane[d * tiles : (d + 1) * tiles]
+        if i == 0:
+            pl.semaphore_wait(barrier, (hops + 1) * n_chan)
+        for turn in range(hops + 1):
+            j = place(turn)
+            for step in range(n_chan):
+                to = lax.rem(chan + step, n_chan)
+                copy = direct(j, step, mine.at[to, i], parts_ref.at[2 * j, chan, i])
+                if step:
+                    copy.start()
+                else:
+                    pl.when(j != 0)(copy.start)
     keep.start()
-    for step in range(n_chan):
-        for j in range(hops, -1, -1):
-            if j or step:
-                direct(j, step).start()
-    keep.wait()
+
+    for turn in range(hops + 1):
+        j = place(turn)
+        for step in range(n_chan):
+            origin = lax.rem(chan + n_chan - step, n_chan)
+            if step:
+                arrival(2 * j, origin).wait_recv()
+            else:
+                pl.when(j == 0)(keep.wait)
+                pl.when(j != 0)(arrival(2 * j, origin).wait_recv)
+            if turn < hops:
+                passed(turn, step).start()
+
+    for turn in range(hops):
+        for step in range(n_chan):
+            arrival(2 * turn + 1, lax.rem(chan + step, n_chan)).wait_recv()
+            passed(turn, step).wait_send()
     for j in range(hops + 1):
         for step in range(n_chan):
             if j or step:
-                arrival(2 * j, lax.rem(chan + n_chan - step, n_chan)).wait_recv()
-        first = j == 0
-        last = j == hops
-
-        @pl.when(odd == 0)
-        def _():
-            if not last:
-                for step in range(n_chan):
-                    passed(j, step).start()
-
-        @pl.when(odd == 1)
-        def _():
-            if not first:
-                for step in range(n_chan):
-                    passed(j - 1, step).start()
-
-    for j in range(hops):
-        for step in range(n_chan):
-            arrival(2 * j + 1, lax.rem(chan + step, n_chan)).wait_recv()
-            passed(j, step).wait_send()
-    for j in range(hops + 1):
-        for step in range(n_chan):
-            if j or step:
-                direct(j, step).wait_send()
+                direct(j, step, mine.at[0], parts_ref.at[0, 0]).wait_send()
 
 
 def channelise(samples, n_chan, half):
@@ -193,11 +199,14 @@
     return pl.pallas_call(
         send_kernel,
         out_shape=jax.ShapeDtypeStruct((half + 1,) + piece, jnp.bfloat16),
-        in_specs=[pl.BlockSpec(memory_space=pltpu.VMEM)] * 6,
+        in_specs=[pl.BlockSpec(memory_space=pl.ANY)] * 2 + [pl.BlockSpec(memory_space=pltpu.VMEM)] * 4,
         out_specs=pl.BlockSpec(memory_space=OUT_SPACE),
         scratch_shapes=[
-            pltpu.VMEM((2 * n_1, inputs * frames * LANES), jnp.float32),
+            pltpu.VMEM(x.shape, jnp.bfloat16),
+            pltpu.VMEM(consts[0].shape, jnp.float32),
+            pltpu.VMEM((2 * n_1, frames * LANES), jnp.float32),
             pltpu.VMEM(piece, jnp.bfloat16),
+            pltpu.SemaphoreType.DMA((inputs + 1,)),
             pltpu.SemaphoreType.DMA,
             pltpu.SemaphoreType.DMA((half // 2 + 1, n_chan)),
             pltpu.SemaphoreType.DMA((half // 2, n_chan)),

time: 21.9 us -> 22.7 us (1.037)
  Pallas kernels: 21.8 us -> 22.5 us
    pallas_call x1, Pallas kernels: 18.5 us -> 19.2 us  [channelise(): pl.pallas_call(send_kernel, out_shape=jax.ShapeDtypeStruct((half + 1,) +...]
where the time goes in v3:
time: 22.7 us; the launch traced here: 22.5 us
  Pallas kernels  22.5 us (99%)
    pallas_call x1, Pallas kernels, channelise(): pl.pallas_call(send_kernel, out_shape=jax.ShapeDtypeStruct((half + 1,) +...  19.2 us
    pallas_call x1, Pallas kernels, correlate(): pl.pallas_call(correlate_kernel, out_shape=jax.ShapeDtypeStruct((inputs,...  3.29 us

profile of v3, /device:TPU:0, one launch (start us, length us, event | category | flops | bytes accessed | tf_op | source)
XLA Modules:
  0.0 22.5 jit_solution(544249669858214462)
XLA Ops:
  0.0 19.2 %channelise.1.parts_ref = bf16[5,4,2,2,2,8,128]{6,5,4,3,2,1,0:T(8,128)(2,1)} custom-call(bf16[2,17,128,128]{3,2,1,0:T(8,128)(2,1)} %bitcast.6, f32[16,128,128]{2,1,0:T(8,128)} %constant.10.clone.taps_ref, f32[128,128]{1,0:T(8,128)} %constant.11.clone.first_ref, f32[128,128]{1,0:T(8,128)} %constant.12.clone.turn_c_ref, f32[128,128]{1,0:T(8,128)} %constant.13.clone.turn_s_ref, ...), custom_call_target="tpu_custom_call" | custom-call | tf_op jit(solution)/shard_map/channelise/pallas_call | solution.py:199
  19.2 3.3 %correlate.1 = bf16[8,2,40,1024]{3,2,1,0:T(8,128)(2,1)} custom-call(s32[8,8]{1,0:T(8,128)} %keeper_ref.1, bf16[5,4,2,2,2,8,128]{6,5,4,3,2,1,0:T(8,128)(2,1)} %channelise.1.parts_ref), custom_call_target="tpu_custom_call" | custom-call | tf_op jit(solution)/shard_map/correlate/pallas_call | solution.py:280

commit v4 on v2

--- a/solution.py
+++ b/solution.py
@@ -212,6 +212,7 @@
     step = pl.program_id(0)
     _, n_chan, pieces, frames, _, tiles, _ = parts_ref.shape
     inputs = n_chan * pieces
+    pieces = out_ref.shape[0]
     slots = parts_ref.shape[0]
     n_stn = keeper_ref.shape[0]
 
@@ -271,12 +272,12 @@
     out = pl.pallas_call(
         correlate_kernel,
         out_shape=jax.ShapeDtypeStruct((inputs, 2, slots * inputs, tiles * LANES), jnp.bfloat16),
-        grid=(n_chan,),
+        grid=(2,),
         in_specs=[
             pl.BlockSpec(memory_space=pltpu.SMEM),
             pl.BlockSpec(parts.shape, lambda t: (0,) * 7),
         ],
-        out_specs=pl.BlockSpec((pieces, 2, slots * inputs, tiles * LANES), lambda t: (t, 0, 0, 0)),
+        out_specs=pl.BlockSpec((inputs // 2, 2, slots * inputs, tiles * LANES), lambda t: (t, 0, 0, 0)),
         scratch_shapes=[
             pltpu.VMEM((frames, 2, tiles, inputs, LANES), jnp.float32),
             pltpu.VMEM((frames, 2, slots, tiles, inputs, LANES), jnp.float32),

time: 21.9 us -> 21.5 us (0.982)
  Pallas kernels: 21.8 us -> 21.3 us
    pallas_call x1, Pallas kernels: 3.29 us -> 2.83 us  [correlate(): pl.pallas_call(correlate_kernel, out_shape=jax.ShapeDtypeStruct((inputs,...]
where the time goes in v4:
time: 21.5 us; the launch traced here: 21.3 us
  Pallas kernels  21.3 us (99%)
    pallas_call x1, Pallas kernels, channelise(): pl.pallas_call(send_kernel, out_shape=jax.ShapeDtypeStruct((half + 1,) +...  18.5 us
    pallas_call x1, Pallas kernels, correlate(): pl.pallas_call(correlate_kernel, out_shape=jax.ShapeDtypeStruct((inputs,...  2.83 us

profile of v4, /device:TPU:0, one launch (start us, length us, event | category | flops | bytes accessed | tf_op | source)
XLA Modules:
  0.0 21.3 jit_solution(5999508366966820523)
XLA Ops:
  0.0 18.5 %channelise.1.parts_ref = bf16[5,4,2,2,2,8,128]{6,5,4,3,2,1,0:T(8,128)(2,1)} custom-call(bf16[2,17,128,128]{3,2,1,0:T(8,128)(2,1)} %bitcast.6, f32[16,128,128]{2,1,0:T(8,128)} %constant.10.clone.taps_ref, f32[128,128]{1,0:T(8,128)} %constant.11.clone.first_ref, f32[128,128]{1,0:T(8,128)} %constant.12.clone.turn_c_ref, f32[128,128]{1,0:T(8,128)} %constant.13.clone.turn_s_ref, ...), custom_call_target="tpu_custom_call" | custom-call | tf_op jit(solution)/shard_map/channelise/pallas_call | solution.py:193
  18.5 2.8 %correlate.1 = bf16[8,2,40,1024]{3,2,1,0:T(8,128)(2,1)} custom-call(s32[8,8]{1,0:T(8,128)} %keeper_ref.1, bf16[5,4,2,2,2,8,128]{6,5,4,3,2,1,0:T(8,128)(2,1)} %channelise.1.parts_ref), custom_call_target="tpu_custom_call" | custom-call | tf_op jit(solution)/shard_map/correlate/pallas_call | solution.py:272
